TPU v7x, 32 devices: a whole 2x2x4 slice. The times are simulated.
32 devices in a mesh: tm: 4 (over z), space: 8 (over y, x, core).
Axes of the slice: x: 2, y: 2, z: 4, core: 2. Of those that a mesh axis runs over, the one named last changes fastest.
Arguments:
- c_state: float32 [4, 2, 64, 2048], P('tm', None, 'space'), may hold values from -4 to 4
Outputs:
- next_state: float32 [4, 2, 64, 2048], P('tm', None, 'space')
All inputs are finite; a program needn't handle non-finite values.
Results may differ from a plain program's by a relative error of at most 0.00002.
Values sent between devices are 32-bit elements; how exact they have to be, the bound alone decides.
No kernel may reach another device: no remote copies, remote signals or barrier semaphores. Data moves between devices by JAX's collectives and lax.ppermute only.
A program may use at most 64 MiB of HBM per device.

v0:
```python
import jax
import jax.numpy as jnp
from jax import lax
from jax.sharding import PartitionSpec as P

FSTEPS = 4
CF = 4
COURANT = 0.06
DIFFUSION = 0.04


def padded_2(block, sides, width):
    for axis, dim in sides:
        count = lax.axis_size(axis)
        forward = [(i, i + 1) for i in range(count - 1)]
        forward.append((count - 1, 0))
        backward = [(target, source) for source, target in forward]
        low = lax.ppermute(
            lax.slice_in_dim(block, block.shape[dim] - width, None, axis=dim), axis, forward
        )
        high = lax.ppermute(lax.slice_in_dim(block, 0, width, axis=dim), axis, backward)
        block = jnp.concatenate([low, block, high], axis=dim)
    return block


def advance(padded, courant, diffusion):
    center = padded[:, 1:-1]
    row_above = padded[:, :-2]
    row_below = padded[:, 2:]
    col_left = jnp.roll(center, 1, axis=2)
    col_right = jnp.roll(center, -1, axis=2)
    along_u = center[0:1]
    along_v = center[1:2]
    transport = jnp.maximum(along_u, 0.0) * (center - row_above) + jnp.minimum(along_u, 0.0) * (
        row_below - center
    )
    transport = (
        transport
        + jnp.maximum(along_v, 0.0) * (center - col_left)
        + jnp.minimum(along_v, 0.0) * (col_right - center)
    )
    spread = row_above + row_below + col_left + col_right - 4.0 * center
    return center - courant * transport + diffusion * spread


def restrict(field):
    blocks = field.reshape(field.shape[0], field.shape[1] // CF, CF, field.shape[2] // CF, CF)
    return jnp.mean(blocks, axis=(2, 4))


def prolong(field):
    return jnp.repeat(jnp.repeat(field, CF, axis=1), CF, axis=2)


def coarse_step(field):
    padded = padded_2(field, (("space", 1),), 1)
    return advance(padded, COURANT * FSTEPS / CF, DIFFUSION * FSTEPS / (CF * CF))


def body(c_state):
    field = c_state[0]
    for section_index in range(FSTEPS):
        padded = padded_2(field, (("space", 1),), 1)
        field = advance(padded, COURANT, DIFFUSION)
    start_coarse = restrict(c_state[0])
    end_coarse = restrict(field)
    defect = end_coarse - coarse_step(start_coarse)
    group_index = lax.axis_index("tm")
    all_start, all_defect = (
        lax.all_gather(start_coarse[None], "tm", axis=0, tiled=True),
        lax.all_gather(defect[None], "tm", axis=0, tiled=True),
    )

    def chain_step(carry, defect_term):
        advanced = coarse_step(carry) + defect_term
        return (advanced, advanced)

    unused, coarse_path = lax.scan(chain_step, all_start[0], all_defect)
    reached = lax.dynamic_index_in_dim(coarse_path, group_index, 0, keepdims=False)
    next_state = field + prolong(reached - end_coarse)
    return next_state[None]


def solution(mesh):
    placed = (P("tm", None, "space", None),)
    return jax.shard_map(
        body, mesh=mesh, in_specs=placed, out_specs=P("tm", None, "space", None), check_vma=False
    )
```

profile of v0, /device:TPU:0, one launch (start us, length us, event | category | flops | bytes accessed | tf_op | source)
XLA Modules:
  0.0 84.8 jit_solution(13688418001067768919)
XLA Ops:
  0.0 1.0 %fusion.74 = (f32[2,1,2048]{2,1,0:T(1,128)S(1)}, f32[2,1,2048]{2,1,0:T(1,128)S(1)}) fusion(f32[2,8,2048]{2,1,0:T(8,128)} %bitcast.68), kind=kLoop, calls=%fused_computation.128 | loop fusion | bytes 65536 | tf_op jit(solution)/shard_map/slice | solution.py:19
  1.0 0.5 collective-permute-start.2
  1.6 2.9 %collective-permute-start.3 = (f32[2,1,2048]{2,0,1:T(2,128)S(1)}, f32[2,1,2048]{2,0,1:T(2,128)S(1)}, u32[]{:S(2)}, u32[]{:S(2)}) collective-permute-start(f32[2,1,2048]{2,0,1:T(2,128)S(1)} %copy.154), channel_id=1, source_target_pairs={{1,0},{2,1},{3,2},{4,3},{5,4},{6,5},{7,6},{0,7},{9,8},{10,9},{11,1... | collective-permute-start | bytes 49160 | tf_op jit(solution)/shard_map/ppermute | solution.py:21
  4.5 6.5 %reshape_squeeze.3 = f32[2,2,4,512,4]{4,3,2,1,0:T(8,128)} reshape(f32[1,2,8,2048]{3,2,1,0:T(8,128)} %param.3) | data formatting | bytes 262144 | tf_op jit(solution)/shard_map/reshape;squeeze | solution.py:47
  11.0 2.5 %reduce_sum.18 = f32[2,2,512]{2,1,0:T(2,128)S(1)} reduce(f32[2,2,4,512,4]{4,3,2,1,0:T(8,128)} %reshape_squeeze.3, f32[]{:T(128)} %constant.9.clone.1), dimensions={2,4}, to_apply=%region_0.1 | reduce | flops 30720 | bytes 139268 | tf_op jit(solution)/shard_map/reduce_sum | solution.py:48
  13.6 0.1 collective-permute-start.10
  13.7 2.6 %collective-permute-start.11 = (f32[2,1,512]{2,1,0:T(1,128)S(1)}, f32[2,1,512]{2,1,0:T(1,128)S(1)}, u32[]{:S(2)}, u32[]{:S(2)}) collective-permute-start(f32[2,1,512]{2,1,0:T(1,128)S(1)} %get-tuple-element.93), channel_id=1, source_target_pairs={{1,0},{2,1},{3,2},{4,3},{5,4},{6,5},{7,6},{0,7},{9,8},{10,9},{11,1... | collective-permute-start | bytes 12296 | tf_op jit(solution)/shard_map/ppermute | solution.py:21
  16.3 0.1 fusion.73
  16.4 0.1 fusion.72
  16.5 0.1 fusion.77
  16.6 0.1 fusion.76
  16.7 14.1 %all-gather = f32[8,2,512]{2,1,0:T(2,128)S(1)} all-gather(f32[2,2,512]{2,1,0:T(2,128)S(1)} %broadcast_multiply_fusion), channel_id=2, replica_groups=mesh['tm'=4,'space'=8] {'tm'}, dimensions={0}, use_global_device_ids=true | all-gather | bytes 40960 | tf_op jit(solution)/shard_map/all_gather | solution.py:70
  30.8 0.2 fusion.51
  31.0 0.1 fusion.70
  31.3 2.7 %collective-permute-start.5 = (f32[2,1,2048]{2,0,1:T(2,128)S(1)}, f32[2,1,2048]{2,0,1:T(2,128)S(1)}, u32[]{:S(2)}, u32[]{:S(2)}) collective-permute-start(f32[2,1,2048]{2,0,1:T(2,128)S(1)} %copy.158), channel_id=1, source_target_pairs={{1,0},{2,1},{3,2},{4,3},{5,4},{6,5},{7,6},{0,7},{9,8},{10,9},{11,1... | collective-permute-start | bytes 49160 | tf_op jit(solution)/shard_map/ppermute | solution.py:21
  33.9 0.1 fusion.69
  34.0 1.3 %collective-permute-done.4 = f32[2,1,2048]{2,0,1:T(2,128)S(1)} collective-permute-done((f32[2,1,2048]{2,0,1:T(2,128)S(1)}, f32[2,1,2048]{2,0,1:T(2,128)S(1)}, u32[]{:S(2)}, u32[]{:S(2)}) %collective-permute-start.4) | collective-permute-done | bytes 16416 | tf_op jit(solution)/shard_map/ppermute | solution.py:18
  35.4 0.2 fusion.36
  35.6 0.1 fusion.67
  35.8 2.7 %collective-permute-start.7 = (f32[2,1,2048]{2,0,1:T(2,128)S(1)}, f32[2,1,2048]{2,0,1:T(2,128)S(1)}, u32[]{:S(2)}, u32[]{:S(2)}) collective-permute-start(f32[2,1,2048]{2,0,1:T(2,128)S(1)} %copy.162), channel_id=1, source_target_pairs={{1,0},{2,1},{3,2},{4,3},{5,4},{6,5},{7,6},{0,7},{9,8},{10,9},{11,1... | collective-permute-start | bytes 49160 | tf_op jit(solution)/shard_map/ppermute | solution.py:21
  38.5 0.1 fusion.66
  38.6 1.3 %collective-permute-done.6 = f32[2,1,2048]{2,0,1:T(2,128)S(1)} collective-permute-done((f32[2,1,2048]{2,0,1:T(2,128)S(1)}, f32[2,1,2048]{2,0,1:T(2,128)S(1)}, u32[]{:S(2)}, u32[]{:S(2)}) %collective-permute-start.6) | collective-permute-done | bytes 16416 | tf_op jit(solution)/shard_map/ppermute | solution.py:18
  39.9 0.1 collective-permute-done.7
  40.0 0.2 fusion.21
  40.2 0.1 fusion.64
  40.3 0.6 collective-permute-start.8
  40.9 2.1 %collective-permute-start.9 = (f32[2,1,2048]{2,0,1:T(2,128)S(1)}, f32[2,1,2048]{2,0,1:T(2,128)S(1)}, u32[]{:S(2)}, u32[]{:S(2)}) collective-permute-start(f32[2,1,2048]{2,0,1:T(2,128)S(1)} %copy.166), channel_id=1, source_target_pairs={{1,0},{2,1},{3,2},{4,3},{5,4},{6,5},{7,6},{0,7},{9,8},{10,9},{11,1... | collective-permute-start | bytes 49160 | tf_op jit(solution)/shard_map/ppermute | solution.py:21
  43.1 0.1 fusion.63
  43.1 1.3 %collective-permute-done.8 = f32[2,1,2048]{2,0,1:T(2,128)S(1)} collective-permute-done((f32[2,1,2048]{2,0,1:T(2,128)S(1)}, f32[2,1,2048]{2,0,1:T(2,128)S(1)}, u32[]{:S(2)}, u32[]{:S(2)}) %collective-permute-start.8) | collective-permute-done | bytes 16416 | tf_op jit(solution)/shard_map/ppermute | solution.py:18
  44.4 0.1 collective-permute-done.9
  44.5 0.2 fusion.6
  44.7 5.7 %reshape.56 = f32[2,2,4,512,4]{4,3,2,1,0:T(8,128)} reshape(f32[2,8,2048]{2,1,0:T(8,128)S(1)} %fusion.6) | data formatting | bytes 262144 | tf_op jit(solution)/shard_map/reshape | solution.py:47
  50.4 2.5 %reduce_sum.19 = f32[2,2,512]{2,1,0:T(2,128)S(1)} reduce(f32[2,2,4,512,4]{4,3,2,1,0:T(8,128)} %reshape.56, f32[]{:T(128)} %constant.9.clone.1), dimensions={2,4}, to_apply=%region_1.2 | reduce | flops 30720 | bytes 139268 | tf_op jit(solution)/shard_map/reduce_sum | solution.py:48
  52.9 0.1 add_subtract_fusion
  53.0 13.1 %all-gather.1 = f32[8,2,512]{2,1,0:T(2,128)S(1)} all-gather(f32[2,2,512]{2,1,0:T(2,128)S(1)} %add_subtract_fusion), channel_id=3, replica_groups=mesh['tm'=4,'space'=8] {'tm'}, dimensions={0}, use_global_device_ids=true | all-gather | bytes 40960 | tf_op jit(solution)/shard_map/all_gather | solution.py:71
  66.2 16.7 %while.12 = (s32[]{:T(128)}, f32[2,2,512]{2,1,0:T(2,128)S(1)}, f32[4,2,2,512]{3,2,1,0:T(2,128)S(1)}, f32[4,2,2,512]{3,2,1,0:T(2,128)S(1)}, s32[]{:T(128)}) while((s32[]{:T(128)}, f32[2,2,512]{2,1,0:T(2,128)S(1)}, f32[4,2,2,512]{3,2,1,0:T(2,128)S(1)}, f32[4,2,2,512]{3,2,1,0:T(2,128)S(1)}, s32[]{:T(128)}) %tuple.68), condition=%wide.region_3.4_spmd, body=%wide.region_2.3_spmd.sunk | while | flops 55298 | bytes 200857 | solution.py:78
  66.3 0.5 collective-permute-start.1
  66.8 0.1 fusion.82
  66.8 0.1 fusion.81
  66.9 0.7 collective-permute-done
  67.6 2.7 %collective-permute-done.1 = f32[2,1,512]{2,1,0:T(1,128)S(1)} collective-permute-done((f32[2,1,512]{2,1,0:T(1,128)S(1)}, f32[2,1,512]{2,1,0:T(1,128)S(1)}, u32[]{:S(2)}, u32[]{:S(2)}) %collective-permute-start.1) | collective-permute-done | bytes 4128 | tf_op jit(solution)/shard_map/while/body/eval_jaxpr/ppermute | solution.py:18
  70.2 0.1 bitcast_dynamic-update-slice_fusion.2
  70.4 0.5 collective-permute-start.1
  70.9 0.1 fusion.82
  71.0 0.1 fusion.81
  71.1 0.7 collective-permute-done
  71.8 2.7 %collective-permute-done.1 = f32[2,1,512]{2,1,0:T(1,128)S(1)} collective-permute-done((f32[2,1,512]{2,1,0:T(1,128)S(1)}, f32[2,1,512]{2,1,0:T(1,128)S(1)}, u32[]{:S(2)}, u32[]{:S(2)}) %collective-permute-start.1) | collective-permute-done | bytes 4128 | tf_op jit(solution)/shard_map/while/body/eval_jaxpr/ppermute | solution.py:18
  74.4 0.1 bitcast_dynamic-update-slice_fusion.2
  74.6 0.5 collective-permute-start.1
  75.1 0.1 fusion.82
  75.2 0.1 fusion.81
  75.3 0.7 collective-permute-done
  76.0 2.7 %collective-permute-done.1 = f32[2,1,512]{2,1,0:T(1,128)S(1)} collective-permute-done((f32[2,1,512]{2,1,0:T(1,128)S(1)}, f32[2,1,512]{2,1,0:T(1,128)S(1)}, u32[]{:S(2)}, u32[]{:S(2)}) %collective-permute-start.1) | collective-permute-done | bytes 4128 | tf_op jit(solution)/shard_map/while/body/eval_jaxpr/ppermute | solution.py:18
  78.6 0.1 bitcast_dynamic-update-slice_fusion.2
  78.8 0.5 collective-permute-start.1
  79.3 0.1 fusion.82
  79.4 0.1 fusion.81
  79.5 0.7 collective-permute-done
  80.1 2.7 %collective-permute-done.1 = f32[2,1,512]{2,1,0:T(1,128)S(1)} collective-permute-done((f32[2,1,512]{2,1,0:T(1,128)S(1)}, f32[2,1,512]{2,1,0:T(1,128)S(1)}, u32[]{:S(2)}, u32[]{:S(2)}) %collective-permute-start.1) | collective-permute-done | bytes 4128 | tf_op jit(solution)/shard_map/while/body/eval_jaxpr/ppermute | solution.py:18
  82.8 0.1 bitcast_dynamic-update-slice_fusion.2
  83.0 0.2 copy.169
  83.2 0.4 broadcast_in_dim.23
  83.5 0.6 copy.170
  84.1 0.7 add_bitcast_fusion
  (56 shorter events, 0.9 us)
Async XLA Ops:
  1.0 29.8 %collective-permute-start.2 = (f32[2,1,2048]{2,0,1:T(2,128)S(1)}, f32[2,1,2048]{2,0,1:T(2,128)S(1)}, u32[]{:S(2)}, u32[]{:S(2)}) collective-permute-start(f32[2,1,2048]{2,0,1:T(2,128)S(1)} %copy.152), channel_id=1, source_target_pairs={{0,1},{1,2},{2,3},{3,4},{4,5},{5,6},{6,7},{7,0},{8,9},{9,10},{10,1... | collective-permute-start | bytes 49160 | tf_op jit(solution)/shard_map/ppermute | solution.py:18
  1.6 14.7 %copy-start = (f32[1,2,8,2048]{3,2,1,0:T(8,128)S(1)}, f32[1,2,8,2048]{3,2,1,0:T(8,128)}, u32[]{:S(2)}) copy-start(f32[1,2,8,2048]{3,2,1,0:T(8,128)} %param.3) | copy-start | bytes 393220
  1.6 29.2 %collective-permute-start.3 = (f32[2,1,2048]{2,0,1:T(2,128)S(1)}, f32[2,1,2048]{2,0,1:T(2,128)S(1)}, u32[]{:S(2)}, u32[]{:S(2)}) collective-permute-start(f32[2,1,2048]{2,0,1:T(2,128)S(1)} %copy.154), channel_id=1, source_target_pairs={{1,0},{2,1},{3,2},{4,3},{5,4},{6,5},{7,6},{0,7},{9,8},{10,9},{11,1... | collective-permute-start | bytes 49160 | tf_op jit(solution)/shard_map/ppermute | solution.py:21
  13.6 39.3 %collective-permute-start.10 = (f32[2,1,512]{2,1,0:T(1,128)S(1)}, f32[2,1,512]{2,1,0:T(1,128)S(1)}, u32[]{:S(2)}, u32[]{:S(2)}) collective-permute-start(f32[2,1,512]{2,1,0:T(1,128)S(1)} %get-tuple-element.92), channel_id=1, source_target_pairs={{0,1},{1,2},{2,3},{3,4},{4,5},{5,6},{6,7},{7,0},{8,9},{9,10},{10,1... | collective-permute-start | bytes 12296 | tf_op jit(solution)/shard_map/ppermute | solution.py:18
  13.7 39.3 %collective-permute-start.11 = (f32[2,1,512]{2,1,0:T(1,128)S(1)}, f32[2,1,512]{2,1,0:T(1,128)S(1)}, u32[]{:S(2)}, u32[]{:S(2)}) collective-permute-start(f32[2,1,512]{2,1,0:T(1,128)S(1)} %get-tuple-element.93), channel_id=1, source_target_pairs={{1,0},{2,1},{3,2},{4,3},{5,4},{6,5},{7,6},{0,7},{9,8},{10,9},{11,1... | collective-permute-start | bytes 12296 | tf_op jit(solution)/shard_map/ppermute | solution.py:21
  31.2 4.2 %collective-permute-start.4 = (f32[2,1,2048]{2,0,1:T(2,128)S(1)}, f32[2,1,2048]{2,0,1:T(2,128)S(1)}, u32[]{:S(2)}, u32[]{:S(2)}) collective-permute-start(f32[2,1,2048]{2,0,1:T(2,128)S(1)} %copy.156), channel_id=1, source_target_pairs={{0,1},{1,2},{2,3},{3,4},{4,5},{5,6},{6,7},{7,0},{8,9},{9,10},{10,1... | collective-permute-start | bytes 49160 | tf_op jit(solution)/shard_map/ppermute | solution.py:18
  31.3 4.1 %collective-permute-start.5 = (f32[2,1,2048]{2,0,1:T(2,128)S(1)}, f32[2,1,2048]{2,0,1:T(2,128)S(1)}, u32[]{:S(2)}, u32[]{:S(2)}) collective-permute-start(f32[2,1,2048]{2,0,1:T(2,128)S(1)} %copy.158), channel_id=1, source_target_pairs={{1,0},{2,1},{3,2},{4,3},{5,4},{6,5},{7,6},{0,7},{9,8},{10,9},{11,1... | collective-permute-start | bytes 49160 | tf_op jit(solution)/shard_map/ppermute | solution.py:21
  35.7 4.1 %collective-permute-start.6 = (f32[2,1,2048]{2,0,1:T(2,128)S(1)}, f32[2,1,2048]{2,0,1:T(2,128)S(1)}, u32[]{:S(2)}, u32[]{:S(2)}) collective-permute-start(f32[2,1,2048]{2,0,1:T(2,128)S(1)} %copy.160), channel_id=1, source_target_pairs={{0,1},{1,2},{2,3},{3,4},{4,5},{5,6},{6,7},{7,0},{8,9},{9,10},{10,1... | collective-permute-start | bytes 49160 | tf_op jit(solution)/shard_map/ppermute | solution.py:18
  35.8 4.1 %collective-permute-start.7 = (f32[2,1,2048]{2,0,1:T(2,128)S(1)}, f32[2,1,2048]{2,0,1:T(2,128)S(1)}, u32[]{:S(2)}, u32[]{:S(2)}) collective-permute-start(f32[2,1,2048]{2,0,1:T(2,128)S(1)} %copy.162), channel_id=1, source_target_pairs={{1,0},{2,1},{3,2},{4,3},{5,4},{6,5},{7,6},{0,7},{9,8},{10,9},{11,1... | collective-permute-start | bytes 49160 | tf_op jit(solution)/shard_map/ppermute | solution.py:21
  40.3 4.1 %collective-permute-start.8 = (f32[2,1,2048]{2,0,1:T(2,128)S(1)}, f32[2,1,2048]{2,0,1:T(2,128)S(1)}, u32[]{:S(2)}, u32[]{:S(2)}) collective-permute-start(f32[2,1,2048]{2,0,1:T(2,128)S(1)} %copy.164), channel_id=1, source_target_pairs={{0,1},{1,2},{2,3},{3,4},{4,5},{5,6},{6,7},{7,0},{8,9},{9,10},{10,1... | collective-permute-start | bytes 49160 | tf_op jit(solution)/shard_map/ppermute | solution.py:18
  40.9 3.6 %collective-permute-start.9 = (f32[2,1,2048]{2,0,1:T(2,128)S(1)}, f32[2,1,2048]{2,0,1:T(2,128)S(1)}, u32[]{:S(2)}, u32[]{:S(2)}) collective-permute-start(f32[2,1,2048]{2,0,1:T(2,128)S(1)} %copy.166), channel_id=1, source_target_pairs={{1,0},{2,1},{3,2},{4,3},{5,4},{6,5},{7,6},{0,7},{9,8},{10,9},{11,1... | collective-permute-start | bytes 49160 | tf_op jit(solution)/shard_map/ppermute | solution.py:21
  66.2 1.4 %collective-permute-start = (f32[2,1,512]{2,1,0:T(1,128)S(1)}, f32[2,1,512]{2,1,0:T(1,128)S(1)}, u32[]{:S(2)}, u32[]{:S(2)}) collective-permute-start(f32[2,1,512]{2,1,0:T(1,128)S(1)} %get-tuple-element.141), channel_id=1, source_target_pairs={{1,0},{2,1},{3,2},{4,3},{5,4},{6,5},{7,6},{0,7},{9,8},{10,9},{11,1... | collective-permute-start | bytes 12296 | tf_op jit(solution)/shard_map/while/body/eval_jaxpr/ppermute | solution.py:21
  66.3 4.0 %collective-permute-start.1 = (f32[2,1,512]{2,1,0:T(1,128)S(1)}, f32[2,1,512]{2,1,0:T(1,128)S(1)}, u32[]{:S(2)}, u32[]{:S(2)}) collective-permute-start(f32[2,1,512]{2,1,0:T(1,128)S(1)} %get-tuple-element.143), channel_id=1, source_target_pairs={{0,1},{1,2},{2,3},{3,4},{4,5},{5,6},{6,7},{7,0},{8,9},{9,10},{10,1... | collective-permute-start | bytes 12296 | tf_op jit(solution)/shard_map/while/body/eval_jaxpr/ppermute | solution.py:18
  70.4 1.4 %collective-permute-start = (f32[2,1,512]{2,1,0:T(1,128)S(1)}, f32[2,1,512]{2,1,0:T(1,128)S(1)}, u32[]{:S(2)}, u32[]{:S(2)}) collective-permute-start(f32[2,1,512]{2,1,0:T(1,128)S(1)} %get-tuple-element.141), channel_id=1, source_target_pairs={{1,0},{2,1},{3,2},{4,3},{5,4},{6,5},{7,6},{0,7},{9,8},{10,9},{11,1... | collective-permute-start | bytes 12296 | tf_op jit(solution)/shard_map/while/body/eval_jaxpr/ppermute | solution.py:21
  70.4 4.0 %collective-permute-start.1 = (f32[2,1,512]{2,1,0:T(1,128)S(1)}, f32[2,1,512]{2,1,0:T(1,128)S(1)}, u32[]{:S(2)}, u32[]{:S(2)}) collective-permute-start(f32[2,1,512]{2,1,0:T(1,128)S(1)} %get-tuple-element.143), channel_id=1, source_target_pairs={{0,1},{1,2},{2,3},{3,4},{4,5},{5,6},{6,7},{7,0},{8,9},{9,10},{10,1... | collective-permute-start | bytes 12296 | tf_op jit(solution)/shard_map/while/body/eval_jaxpr/ppermute | solution.py:18
  74.6 1.4 %collective-permute-start = (f32[2,1,512]{2,1,0:T(1,128)S(1)}, f32[2,1,512]{2,1,0:T(1,128)S(1)}, u32[]{:S(2)}, u32[]{:S(2)}) collective-permute-start(f32[2,1,512]{2,1,0:T(1,128)S(1)} %get-tuple-element.141), channel_id=1, source_target_pairs={{1,0},{2,1},{3,2},{4,3},{5,4},{6,5},{7,6},{0,7},{9,8},{10,9},{11,1... | collective-permute-start | bytes 12296 | tf_op jit(solution)/shard_map/while/body/eval_jaxpr/ppermute | solution.py:21
  74.6 4.0 %collective-permute-start.1 = (f32[2,1,512]{2,1,0:T(1,128)S(1)}, f32[2,1,512]{2,1,0:T(1,128)S(1)}, u32[]{:S(2)}, u32[]{:S(2)}) collective-permute-start(f32[2,1,512]{2,1,0:T(1,128)S(1)} %get-tuple-element.143), channel_id=1, source_target_pairs={{0,1},{1,2},{2,3},{3,4},{4,5},{5,6},{6,7},{7,0},{8,9},{9,10},{10,1... | collective-permute-start | bytes 12296 | tf_op jit(solution)/shard_map/while/body/eval_jaxpr/ppermute | solution.py:18
  78.8 1.4 %collective-permute-start = (f32[2,1,512]{2,1,0:T(1,128)S(1)}, f32[2,1,512]{2,1,0:T(1,128)S(1)}, u32[]{:S(2)}, u32[]{:S(2)}) collective-permute-start(f32[2,1,512]{2,1,0:T(1,128)S(1)} %get-tuple-element.141), channel_id=1, source_target_pairs={{1,0},{2,1},{3,2},{4,3},{5,4},{6,5},{7,6},{0,7},{9,8},{10,9},{11,1... | collective-permute-start | bytes 12296 | tf_op jit(solution)/shard_map/while/body/eval_jaxpr/ppermute | solution.py:21
  78.8 4.0 %collective-permute-start.1 = (f32[2,1,512]{2,1,0:T(1,128)S(1)}, f32[2,1,512]{2,1,0:T(1,128)S(1)}, u32[]{:S(2)}, u32[]{:S(2)}) collective-permute-start(f32[2,1,512]{2,1,0:T(1,128)S(1)} %get-tuple-element.143), channel_id=1, source_target_pairs={{0,1},{1,2},{2,3},{3,4},{4,5},{5,6},{6,7},{7,0},{8,9},{9,10},{10,1... | collective-permute-start | bytes 12296 | tf_op jit(solution)/shard_map/while/body/eval_jaxpr/ppermute | solution.py:18
where the time goes:
time: 85.1 us; the launch traced here: 84.8 us
  blocking collectives  27.3 us (32%)
  waiting for transfers between devices  17.4 us (20%)
  starting transfers between devices  16.6 us (20%)
  local copies, waits for them, and re-layouts  16 us (19%)
  other arithmetic  7.04 us (8%)
    ppermute x9, waiting for transfers between devices, padded_2(): lax.ppermute(lax.slice_in_dim(block, block.shape[dim] - width, None, axis...  14.6 us
    all_gather x1, blocking collectives, body(): lax.all_gather(start_coarse[None], 'tm', axis=0, tiled=True)  14.1 us
    ppermute x9, starting transfers between devices, padded_2(): lax.ppermute(lax.slice_in_dim(block, 0, width, axis=dim), axis, backward)  13.3 us
    all_gather x1, blocking collectives, body(): lax.all_gather(defect[None], 'tm', axis=0, tiled=True)  13.1 us
    another operation x1, local copies, waits for them, and re-layouts, restrict(): field.reshape(field.shape[0], field.shape[1] // CF, CF, field.shape[2] //...  6.49 us
    reshape x1, local copies, waits for them, and re-layouts, restrict(): field.reshape(field.shape[0], field.shape[1] // CF, CF, field.shape[2] //...  5.67 us
    reduce_sum x2, other arithmetic, restrict(): return jnp.mean(blocks, axis=(2, 4))  5.09 us
    ppermute x9, starting transfers between devices, padded_2(): lax.ppermute(lax.slice_in_dim(block, block.shape[dim] - width, None, axis...  3.32 us
  transfers between devices with their start and end apart: 18, of which 13 were waited for; matrix products, arithmetic and copies ran while one was open for 23% of the time, Pallas kernels for 0%

commit v1 on v0

--- a/solution.py
+++ b/solution.py
@@ -7,6 +7,36 @@
 CF = 4
 COURANT = 0.06
 DIFFUSION = 0.04
+
+
+def point_sides(array_in, dimension_no):
+    array_in = jnp.moveaxis(array_in, 0, dimension_no)
+    reply = array_in.shape
+    return array_in.reshape(
+        *reply[:dimension_no],
+        reply[dimension_no] * reply[dimension_no + 1],
+        *reply[dimension_no + 2 :]
+    )
+
+
+def handle_cycles(page, comm_axis):
+    z_new = page[None]
+    total_devices = lax.axis_size(comm_axis)
+    for idx in range(total_devices.bit_length() - 1):
+        r2 = 1 << idx
+        outer = lax.ppermute(
+            z_new,
+            comm_axis,
+            perm=list(map(lambda dev_j: (dev_j, dev_j ^ r2), range(total_devices))),
+        )
+        met_up = jnp.stack([z_new, outer], axis=0)
+        piece_now = lax.axis_index(comm_axis) >> idx & 1
+        z_new = jnp.where(piece_now == 0, met_up, met_up[::-1]).reshape(-1, *page.shape)
+    return z_new
+
+
+def sheet_hold(local_array, load, row_dim):
+    return point_sides(handle_cycles(local_array, load), row_dim)
 
 
 def padded_2(block, sides, width):
@@ -68,7 +98,7 @@
     group_index = lax.axis_index("tm")
     all_start, all_defect = (
         lax.all_gather(start_coarse[None], "tm", axis=0, tiled=True),
-        lax.all_gather(defect[None], "tm", axis=0, tiled=True),
+        sheet_hold(defect[None], "tm", 0),
     )
 
     def chain_step(carry, defect_term):

time: 85.1 us -> 78.2 us (0.919)
  blocking collectives: 27.3 us -> 13.1 us
  starting transfers between devices: 16.6 us -> 22.1 us
  waiting for transfers between devices: 17.4 us -> 19 us
    all_gather x1 -> x0, blocking collectives: 13.1 us -> none  [body(): lax.all_gather(defect[None], 'tm', axis=0, tiled=True)]
    ppermute x0 -> x2, starting transfers between devices: none -> 5.49 us  [handle_cycles(): lax.ppermute(z_new, comm_axis, perm=list(map(lambda dev_j: (dev_j, dev_j...]
    ppermute x0 -> x2, waiting for transfers between devices: none -> 1.63 us  [handle_cycles(): lax.ppermute(z_new, comm_axis, perm=list(map(lambda dev_j: (dev_j, dev_j...]
    all_gather x1, blocking collectives: 14.1 us -> 13.1 us  [body(): lax.all_gather(start_coarse[None], 'tm', axis=0, tiled=True)]
  transfers between devices with their start and end apart: 18 -> 20, of which waited for: 13 -> 15; matrix products, arithmetic and copies ran while one was open for 23% -> 25% of each run, Pallas kernels for 0% -> 0%
where the time goes in v1:
time: 78.2 us; the launch traced here: 77.9 us
  starting transfers between devices  22.1 us (28%)
  waiting for transfers between devices  19 us (24%)
  local copies, waits for them, and re-layouts  16 us (20%)
  blocking collectives  13.1 us (17%)
  other arithmetic  7.1 us (9%)
    ppermute x9, waiting for transfers between devices, padded_2(): lax.ppermute(lax.slice_in_dim(block, block.shape[dim] - width, None, axis...  14.5 us
    all_gather x1, blocking collectives, body(): lax.all_gather(start_coarse[None], 'tm', axis=0, tiled=True)  13.1 us
    ppermute x9, starting transfers between devices, padded_2(): lax.ppermute(lax.slice_in_dim(block, 0, width, axis=dim), axis, backward)  12.5 us
    another operation x1, local copies, waits for them, and re-layouts, restrict(): field.reshape(field.shape[0], field.shape[1] // CF, CF, field.shape[2] //...  6.49 us
    reshape x1, local copies, waits for them, and re-layouts, restrict(): field.reshape(field.shape[0], field.shape[1] // CF, CF, field.shape[2] //...  5.67 us
    ppermute x2, starting transfers between devices, handle_cycles(): lax.ppermute(z_new, comm_axis, perm=list(map(lambda dev_j: (dev_j, dev_j...  5.49 us
    reduce_sum x2, other arithmetic, restrict(): return jnp.mean(blocks, axis=(2, 4))  5.09 us
    ppermute x9, starting transfers between devices, padded_2(): lax.ppermute(lax.slice_in_dim(block, block.shape[dim] - width, None, axis...  4.12 us
  transfers between devices with their start and end apart: 20, of which 15 were waited for; matrix products, arithmetic and copies ran while one was open for 25% of the time, Pallas kernels for 0%

profile of v1, /device:TPU:0, one launch (start us, length us, event | category | flops | bytes accessed | tf_op | source)
XLA Modules:
  0.0 77.9 jit_solution(10850575216299611679)
XLA Ops:
  0.0 1.0 %fusion.76 = (f32[2,1,2048]{2,1,0:T(1,128)S(1)}, f32[2,1,2048]{2,1,0:T(1,128)S(1)}) fusion(f32[2,8,2048]{2,1,0:T(8,128)} %bitcast.76), kind=kLoop, calls=%fused_computation.134 | loop fusion | bytes 65536 | tf_op jit(solution)/shard_map/slice | solution.py:49
  1.0 0.5 collective-permute-start.2
  1.6 2.9 %collective-permute-start.3 = (f32[2,1,2048]{2,0,1:T(2,128)S(1)}, f32[2,1,2048]{2,0,1:T(2,128)S(1)}, u32[]{:S(2)}, u32[]{:S(2)}) collective-permute-start(f32[2,1,2048]{2,0,1:T(2,128)S(1)} %copy.154), channel_id=1, source_target_pairs={{1,0},{2,1},{3,2},{4,3},{5,4},{6,5},{7,6},{0,7},{9,8},{10,9},{11,1... | collective-permute-start | bytes 49160 | tf_op jit(solution)/shard_map/ppermute | solution.py:51
  4.5 6.5 %reshape_squeeze.3 = f32[2,2,4,512,4]{4,3,2,1,0:T(8,128)} reshape(f32[1,2,8,2048]{3,2,1,0:T(8,128)} %param.3) | data formatting | bytes 262144 | tf_op jit(solution)/shard_map/reshape;squeeze | solution.py:77
  11.0 2.5 %reduce_sum.18 = f32[2,2,512]{2,1,0:T(2,128)S(1)} reduce(f32[2,2,4,512,4]{4,3,2,1,0:T(8,128)} %reshape_squeeze.3, f32[]{:T(128)} %constant.11.clone.1), dimensions={2,4}, to_apply=%region_0.1 | reduce | flops 30720 | bytes 139268 | tf_op jit(solution)/shard_map/reduce_sum | solution.py:78
  13.7 2.6 %collective-permute-start.11 = (f32[2,1,512]{2,1,0:T(1,128)S(1)}, f32[2,1,512]{2,1,0:T(1,128)S(1)}, u32[]{:S(2)}, u32[]{:S(2)}) collective-permute-start(f32[2,1,512]{2,1,0:T(1,128)S(1)} %get-tuple-element.95), channel_id=1, source_target_pairs={{1,0},{2,1},{3,2},{4,3},{5,4},{6,5},{7,6},{0,7},{9,8},{10,9},{11,1... | collective-permute-start | bytes 12296 | tf_op jit(solution)/shard_map/ppermute | solution.py:51
  16.3 0.1 fusion.75
  16.4 0.1 fusion.74
  16.5 0.1 fusion.79
  16.6 0.1 fusion.78
  16.7 0.2 fusion.51
  16.9 0.1 fusion.72
  17.2 2.7 %collective-permute-start.5 = (f32[2,1,2048]{2,0,1:T(2,128)S(1)}, f32[2,1,2048]{2,0,1:T(2,128)S(1)}, u32[]{:S(2)}, u32[]{:S(2)}) collective-permute-start(f32[2,1,2048]{2,0,1:T(2,128)S(1)} %copy.158), channel_id=1, source_target_pairs={{1,0},{2,1},{3,2},{4,3},{5,4},{6,5},{7,6},{0,7},{9,8},{10,9},{11,1... | collective-permute-start | bytes 49160 | tf_op jit(solution)/shard_map/ppermute | solution.py:51
  19.8 0.1 fusion.71
  19.9 1.3 %collective-permute-done.4 = f32[2,1,2048]{2,0,1:T(2,128)S(1)} collective-permute-done((f32[2,1,2048]{2,0,1:T(2,128)S(1)}, f32[2,1,2048]{2,0,1:T(2,128)S(1)}, u32[]{:S(2)}, u32[]{:S(2)}) %collective-permute-start.4) | collective-permute-done | bytes 16416 | tf_op jit(solution)/shard_map/ppermute | solution.py:48
  21.2 0.1 collective-permute-done.5
  21.3 0.2 fusion.36
  21.5 0.1 fusion.69
  21.7 2.7 %collective-permute-start.7 = (f32[2,1,2048]{2,0,1:T(2,128)S(1)}, f32[2,1,2048]{2,0,1:T(2,128)S(1)}, u32[]{:S(2)}, u32[]{:S(2)}) collective-permute-start(f32[2,1,2048]{2,0,1:T(2,128)S(1)} %copy.162), channel_id=1, source_target_pairs={{1,0},{2,1},{3,2},{4,3},{5,4},{6,5},{7,6},{0,7},{9,8},{10,9},{11,1... | collective-permute-start | bytes 49160 | tf_op jit(solution)/shard_map/ppermute | solution.py:51
  24.4 0.1 fusion.68
  24.5 1.3 %collective-permute-done.6 = f32[2,1,2048]{2,0,1:T(2,128)S(1)} collective-permute-done((f32[2,1,2048]{2,0,1:T(2,128)S(1)}, f32[2,1,2048]{2,0,1:T(2,128)S(1)}, u32[]{:S(2)}, u32[]{:S(2)}) %collective-permute-start.6) | collective-permute-done | bytes 16416 | tf_op jit(solution)/shard_map/ppermute | solution.py:48
  25.9 0.2 fusion.21
  26.1 0.1 fusion.66
  26.2 1.4 %collective-permute-start.8 = (f32[2,1,2048]{2,0,1:T(2,128)S(1)}, f32[2,1,2048]{2,0,1:T(2,128)S(1)}, u32[]{:S(2)}, u32[]{:S(2)}) collective-permute-start(f32[2,1,2048]{2,0,1:T(2,128)S(1)} %copy.164), channel_id=1, source_target_pairs={{0,1},{1,2},{2,3},{3,4},{4,5},{5,6},{6,7},{7,0},{8,9},{9,10},{10,1... | collective-permute-start | bytes 49160 | tf_op jit(solution)/shard_map/ppermute | solution.py:48
  27.6 1.3 %collective-permute-start.9 = (f32[2,1,2048]{2,0,1:T(2,128)S(1)}, f32[2,1,2048]{2,0,1:T(2,128)S(1)}, u32[]{:S(2)}, u32[]{:S(2)}) collective-permute-start(f32[2,1,2048]{2,0,1:T(2,128)S(1)} %copy.166), channel_id=1, source_target_pairs={{1,0},{2,1},{3,2},{4,3},{5,4},{6,5},{7,6},{0,7},{9,8},{10,9},{11,1... | collective-permute-start | bytes 49160 | tf_op jit(solution)/shard_map/ppermute | solution.py:51
  29.0 0.1 fusion.65
  29.0 1.3 %collective-permute-done.8 = f32[2,1,2048]{2,0,1:T(2,128)S(1)} collective-permute-done((f32[2,1,2048]{2,0,1:T(2,128)S(1)}, f32[2,1,2048]{2,0,1:T(2,128)S(1)}, u32[]{:S(2)}, u32[]{:S(2)}) %collective-permute-start.8) | collective-permute-done | bytes 16416 | tf_op jit(solution)/shard_map/ppermute | solution.py:48
  30.4 0.2 fusion.6
  30.6 5.7 %reshape.59 = f32[2,2,4,512,4]{4,3,2,1,0:T(8,128)} reshape(f32[2,8,2048]{2,1,0:T(8,128)S(1)} %fusion.6) | data formatting | bytes 262144 | tf_op jit(solution)/shard_map/reshape | solution.py:77
  36.3 2.5 %reduce_sum.19 = f32[2,2,512]{2,1,0:T(2,128)S(1)} reduce(f32[2,2,4,512,4]{4,3,2,1,0:T(8,128)} %reshape.59, f32[]{:T(128)} %constant.11.clone.1), dimensions={2,4}, to_apply=%region_1.2 | reduce | flops 30720 | bytes 139268 | tf_op jit(solution)/shard_map/reduce_sum | solution.py:78
  38.8 0.1 add_subtract_fusion
  38.9 2.4 %collective-permute-start.12 = (f32[1,1,2,2,512]{4,3,2,1,0:T(2,128)S(1)}, f32[1,1,2,2,512]{4,3,2,1,0:T(2,128)S(1)}, u32[]{:S(2)}, u32[]{:S(2)}) collective-permute-start(f32[1,1,2,2,512]{4,3,2,1,0:T(2,128)S(1)} %bitcast.82), channel_id=1, source_target_pairs={{0,8},{8,0},{16,24},{24,16},{1,9},{9,1},{17,25},{25,17},{2,10},{10... | collective-permute-start | bytes 24584 | tf_op jit(solution)/shard_map/ppermute | solution.py:27
  41.3 1.6 %collective-permute-done.12 = f32[1,1,2,2,512]{4,3,2,1,0:T(2,128)S(1)} collective-permute-done((f32[1,1,2,2,512]{4,3,2,1,0:T(2,128)S(1)}, f32[1,1,2,2,512]{4,3,2,1,0:T(2,128)S(1)}, u32[]{:S(2)}, u32[]{:S(2)}) %collective-permute-start.12) | collective-permute-done | bytes 8224 | tf_op jit(solution)/shard_map/ppermute | solution.py:27
  43.0 3.1 %collective-permute-start.13 = (f32[2,1,2,2,512]{4,3,2,0,1:T(2,128)S(1)}, f32[2,1,2,2,512]{4,3,2,0,1:T(2,128)S(1)}, u32[]{:S(2)}, u32[]{:S(2)}) collective-permute-start(f32[2,1,2,2,512]{4,3,2,0,1:T(2,128)S(1)} %get-tuple-element.89), channel_id=1, source_target_pairs={{0,16},{8,24},{16,0},{24,8},{1,17},{9,25},{17,1},{25,9},{2,18},{10... | collective-permute-start | bytes 49160 | tf_op jit(solution)/shard_map/ppermute | solution.py:27
  46.1 13.1 %all-gather = f32[8,2,512]{2,1,0:T(2,128)S(1)} all-gather(f32[2,2,512]{2,1,0:T(2,128)S(1)} %broadcast_multiply_fusion), channel_id=2, replica_groups=mesh['tm'=4,'space'=8] {'tm'}, dimensions={0}, use_global_device_ids=true | all-gather | bytes 40960 | tf_op jit(solution)/shard_map/all_gather | solution.py:100
  59.3 16.8 %while.12 = (s32[]{:T(128)}, f32[2,2,512]{2,1,0:T(2,128)S(1)}, f32[4,2,2,512]{3,2,1,0:T(2,128)S(1)}, f32[4,2,2,512]{3,2,1,0:T(2,128)S(1)}, s32[]{:T(128)}) while((s32[]{:T(128)}, f32[2,2,512]{2,1,0:T(2,128)S(1)}, f32[4,2,2,512]{3,2,1,0:T(2,128)S(1)}, f32[4,2,2,512]{3,2,1,0:T(2,128)S(1)}, s32[]{:T(128)}) %tuple.69), condition=%wide.region_3.4_spmd, body=%wide.region_2.3_spmd.sunk | while | flops 55298 | bytes 200857 | solution.py:108
  59.4 0.5 collective-permute-start.1
  59.9 0.1 fusion.84
  60.0 0.1 fusion.83
  60.0 0.7 collective-permute-done
  60.7 2.7 %collective-permute-done.1 = f32[2,1,512]{2,1,0:T(1,128)S(1)} collective-permute-done((f32[2,1,512]{2,1,0:T(1,128)S(1)}, f32[2,1,512]{2,1,0:T(1,128)S(1)}, u32[]{:S(2)}, u32[]{:S(2)}) %collective-permute-start.1) | collective-permute-done | bytes 4128 | tf_op jit(solution)/shard_map/while/body/eval_jaxpr/ppermute | solution.py:48
  63.4 0.1 bitcast_dynamic-update-slice_fusion.2
  63.6 0.5 collective-permute-start.1
  64.1 0.1 fusion.84
  64.1 0.1 fusion.83
  64.2 0.7 collective-permute-done
  64.9 2.7 %collective-permute-done.1 = f32[2,1,512]{2,1,0:T(1,128)S(1)} collective-permute-done((f32[2,1,512]{2,1,0:T(1,128)S(1)}, f32[2,1,512]{2,1,0:T(1,128)S(1)}, u32[]{:S(2)}, u32[]{:S(2)}) %collective-permute-start.1) | collective-permute-done | bytes 4128 | tf_op jit(solution)/shard_map/while/body/eval_jaxpr/ppermute | solution.py:48
  67.5 0.1 bitcast_dynamic-update-slice_fusion.2
  67.7 0.5 collective-permute-start.1
  68.3 0.1 fusion.84
  68.3 0.1 fusion.83
  68.4 0.7 collective-permute-done
  69.1 2.7 %collective-permute-done.1 = f32[2,1,512]{2,1,0:T(1,128)S(1)} collective-permute-done((f32[2,1,512]{2,1,0:T(1,128)S(1)}, f32[2,1,512]{2,1,0:T(1,128)S(1)}, u32[]{:S(2)}, u32[]{:S(2)}) %collective-permute-start.1) | collective-permute-done | bytes 4128 | tf_op jit(solution)/shard_map/while/body/eval_jaxpr/ppermute | solution.py:48
  71.7 0.1 bitcast_dynamic-update-slice_fusion.2
  71.9 0.5 collective-permute-start.1
  72.4 0.1 fusion.84
  72.5 0.1 fusion.83
  72.6 0.7 collective-permute-done
  73.3 2.7 %collective-permute-done.1 = f32[2,1,512]{2,1,0:T(1,128)S(1)} collective-permute-done((f32[2,1,512]{2,1,0:T(1,128)S(1)}, f32[2,1,512]{2,1,0:T(1,128)S(1)}, u32[]{:S(2)}, u32[]{:S(2)}) %collective-permute-start.1) | collective-permute-done | bytes 4128 | tf_op jit(solution)/shard_map/while/body/eval_jaxpr/ppermute | solution.py:48
  75.9 0.1 bitcast_dynamic-update-slice_fusion.2
  76.1 0.2 copy.169
  76.3 0.4 broadcast_in_dim.19
  76.7 0.6 copy.170
  77.2 0.7 add_bitcast_fusion
  (63 shorter events, 1.1 us)
Async XLA Ops:
  1.0 15.6 %collective-permute-start.2 = (f32[2,1,2048]{2,0,1:T(2,128)S(1)}, f32[2,1,2048]{2,0,1:T(2,128)S(1)}, u32[]{:S(2)}, u32[]{:S(2)}) collective-permute-start(f32[2,1,2048]{2,0,1:T(2,128)S(1)} %copy.152), channel_id=1, source_target_pairs={{0,1},{1,2},{2,3},{3,4},{4,5},{5,6},{6,7},{7,0},{8,9},{9,10},{10,1... | collective-permute-start | bytes 49160 | tf_op jit(solution)/shard_map/ppermute | solution.py:48
  1.6 14.7 %copy-start = (f32[1,2,8,2048]{3,2,1,0:T(8,128)S(1)}, f32[1,2,8,2048]{3,2,1,0:T(8,128)}, u32[]{:S(2)}) copy-start(f32[1,2,8,2048]{3,2,1,0:T(8,128)} %param.3) | copy-start | bytes 393220
  1.6 15.1 %collective-permute-start.3 = (f32[2,1,2048]{2,0,1:T(2,128)S(1)}, f32[2,1,2048]{2,0,1:T(2,128)S(1)}, u32[]{:S(2)}, u32[]{:S(2)}) collective-permute-start(f32[2,1,2048]{2,0,1:T(2,128)S(1)} %copy.154), channel_id=1, source_target_pairs={{1,0},{2,1},{3,2},{4,3},{5,4},{6,5},{7,6},{0,7},{9,8},{10,9},{11,1... | collective-permute-start | bytes 49160 | tf_op jit(solution)/shard_map/ppermute | solution.py:51
  13.6 25.2 %collective-permute-start.10 = (f32[2,1,512]{2,1,0:T(1,128)S(1)}, f32[2,1,512]{2,1,0:T(1,128)S(1)}, u32[]{:S(2)}, u32[]{:S(2)}) collective-permute-start(f32[2,1,512]{2,1,0:T(1,128)S(1)} %get-tuple-element.94), channel_id=1, source_target_pairs={{0,1},{1,2},{2,3},{3,4},{4,5},{5,6},{6,7},{7,0},{8,9},{9,10},{10,1... | collective-permute-start | bytes 12296 | tf_op jit(solution)/shard_map/ppermute | solution.py:48
  13.7 25.2 %collective-permute-start.11 = (f32[2,1,512]{2,1,0:T(1,128)S(1)}, f32[2,1,512]{2,1,0:T(1,128)S(1)}, u32[]{:S(2)}, u32[]{:S(2)}) collective-permute-start(f32[2,1,512]{2,1,0:T(1,128)S(1)} %get-tuple-element.95), channel_id=1, source_target_pairs={{1,0},{2,1},{3,2},{4,3},{5,4},{6,5},{7,6},{0,7},{9,8},{10,9},{11,1... | collective-permute-start | bytes 12296 | tf_op jit(solution)/shard_map/ppermute | solution.py:51
  17.1 4.1 %collective-permute-start.4 = (f32[2,1,2048]{2,0,1:T(2,128)S(1)}, f32[2,1,2048]{2,0,1:T(2,128)S(1)}, u32[]{:S(2)}, u32[]{:S(2)}) collective-permute-start(f32[2,1,2048]{2,0,1:T(2,128)S(1)} %copy.156), channel_id=1, source_target_pairs={{0,1},{1,2},{2,3},{3,4},{4,5},{5,6},{6,7},{7,0},{8,9},{9,10},{10,1... | collective-permute-start | bytes 49160 | tf_op jit(solution)/shard_map/ppermute | solution.py:48
  17.2 4.1 %collective-permute-start.5 = (f32[2,1,2048]{2,0,1:T(2,128)S(1)}, f32[2,1,2048]{2,0,1:T(2,128)S(1)}, u32[]{:S(2)}, u32[]{:S(2)}) collective-permute-start(f32[2,1,2048]{2,0,1:T(2,128)S(1)} %copy.158), channel_id=1, source_target_pairs={{1,0},{2,1},{3,2},{4,3},{5,4},{6,5},{7,6},{0,7},{9,8},{10,9},{11,1... | collective-permute-start | bytes 49160 | tf_op jit(solution)/shard_map/ppermute | solution.py:51
  21.6 4.1 %collective-permute-start.6 = (f32[2,1,2048]{2,0,1:T(2,128)S(1)}, f32[2,1,2048]{2,0,1:T(2,128)S(1)}, u32[]{:S(2)}, u32[]{:S(2)}) collective-permute-start(f32[2,1,2048]{2,0,1:T(2,128)S(1)} %copy.160), channel_id=1, source_target_pairs={{0,1},{1,2},{2,3},{3,4},{4,5},{5,6},{6,7},{7,0},{8,9},{9,10},{10,1... | collective-permute-start | bytes 49160 | tf_op jit(solution)/shard_map/ppermute | solution.py:48
  21.7 4.1 %collective-permute-start.7 = (f32[2,1,2048]{2,0,1:T(2,128)S(1)}, f32[2,1,2048]{2,0,1:T(2,128)S(1)}, u32[]{:S(2)}, u32[]{:S(2)}) collective-permute-start(f32[2,1,2048]{2,0,1:T(2,128)S(1)} %copy.162), channel_id=1, source_target_pairs={{1,0},{2,1},{3,2},{4,3},{5,4},{6,5},{7,6},{0,7},{9,8},{10,9},{11,1... | collective-permute-start | bytes 49160 | tf_op jit(solution)/shard_map/ppermute | solution.py:51
  26.2 4.1 %collective-permute-start.8 = (f32[2,1,2048]{2,0,1:T(2,128)S(1)}, f32[2,1,2048]{2,0,1:T(2,128)S(1)}, u32[]{:S(2)}, u32[]{:S(2)}) collective-permute-start(f32[2,1,2048]{2,0,1:T(2,128)S(1)} %copy.164), channel_id=1, source_target_pairs={{0,1},{1,2},{2,3},{3,4},{4,5},{5,6},{6,7},{7,0},{8,9},{9,10},{10,1... | collective-permute-start | bytes 49160 | tf_op jit(solution)/shard_map/ppermute | solution.py:48
  27.6 2.8 %collective-permute-start.9 = (f32[2,1,2048]{2,0,1:T(2,128)S(1)}, f32[2,1,2048]{2,0,1:T(2,128)S(1)}, u32[]{:S(2)}, u32[]{:S(2)}) collective-permute-start(f32[2,1,2048]{2,0,1:T(2,128)S(1)} %copy.166), channel_id=1, source_target_pairs={{1,0},{2,1},{3,2},{4,3},{5,4},{6,5},{7,6},{0,7},{9,8},{10,9},{11,1... | collective-permute-start | bytes 49160 | tf_op jit(solution)/shard_map/ppermute | solution.py:51
  38.9 4.0 %collective-permute-start.12 = (f32[1,1,2,2,512]{4,3,2,1,0:T(2,128)S(1)}, f32[1,1,2,2,512]{4,3,2,1,0:T(2,128)S(1)}, u32[]{:S(2)}, u32[]{:S(2)}) collective-permute-start(f32[1,1,2,2,512]{4,3,2,1,0:T(2,128)S(1)} %bitcast.82), channel_id=1, source_target_pairs={{0,8},{8,0},{16,24},{24,16},{1,9},{9,1},{17,25},{25,17},{2,10},{10... | collective-permute-start | bytes 24584 | tf_op jit(solution)/shard_map/ppermute | solution.py:27
  43.0 16.2 %collective-permute-start.13 = (f32[2,1,2,2,512]{4,3,2,0,1:T(2,128)S(1)}, f32[2,1,2,2,512]{4,3,2,0,1:T(2,128)S(1)}, u32[]{:S(2)}, u32[]{:S(2)}) collective-permute-start(f32[2,1,2,2,512]{4,3,2,0,1:T(2,128)S(1)} %get-tuple-element.89), channel_id=1, source_target_pairs={{0,16},{8,24},{16,0},{24,8},{1,17},{9,25},{17,1},{25,9},{2,18},{10... | collective-permute-start | bytes 49160 | tf_op jit(solution)/shard_map/ppermute | solution.py:27
  59.3 1.4 %collective-permute-start = (f32[2,1,512]{2,1,0:T(1,128)S(1)}, f32[2,1,512]{2,1,0:T(1,128)S(1)}, u32[]{:S(2)}, u32[]{:S(2)}) collective-permute-start(f32[2,1,512]{2,1,0:T(1,128)S(1)} %get-tuple-element.143), channel_id=1, source_target_pairs={{1,0},{2,1},{3,2},{4,3},{5,4},{6,5},{7,6},{0,7},{9,8},{10,9},{11,1... | collective-permute-start | bytes 12296 | tf_op jit(solution)/shard_map/while/body/eval_jaxpr/ppermute | solution.py:51
  59.4 4.0 %collective-permute-start.1 = (f32[2,1,512]{2,1,0:T(1,128)S(1)}, f32[2,1,512]{2,1,0:T(1,128)S(1)}, u32[]{:S(2)}, u32[]{:S(2)}) collective-permute-start(f32[2,1,512]{2,1,0:T(1,128)S(1)} %get-tuple-element.145), channel_id=1, source_target_pairs={{0,1},{1,2},{2,3},{3,4},{4,5},{5,6},{6,7},{7,0},{8,9},{9,10},{10,1... | collective-permute-start | bytes 12296 | tf_op jit(solution)/shard_map/while/body/eval_jaxpr/ppermute | solution.py:48
  63.5 1.4 %collective-permute-start = (f32[2,1,512]{2,1,0:T(1,128)S(1)}, f32[2,1,512]{2,1,0:T(1,128)S(1)}, u32[]{:S(2)}, u32[]{:S(2)}) collective-permute-start(f32[2,1,512]{2,1,0:T(1,128)S(1)} %get-tuple-element.143), channel_id=1, source_target_pairs={{1,0},{2,1},{3,2},{4,3},{5,4},{6,5},{7,6},{0,7},{9,8},{10,9},{11,1... | collective-permute-start | bytes 12296 | tf_op jit(solution)/shard_map/while/body/eval_jaxpr/ppermute | solution.py:51
  63.6 4.0 %collective-permute-start.1 = (f32[2,1,512]{2,1,0:T(1,128)S(1)}, f32[2,1,512]{2,1,0:T(1,128)S(1)}, u32[]{:S(2)}, u32[]{:S(2)}) collective-permute-start(f32[2,1,512]{2,1,0:T(1,128)S(1)} %get-tuple-element.145), channel_id=1, source_target_pairs={{0,1},{1,2},{2,3},{3,4},{4,5},{5,6},{6,7},{7,0},{8,9},{9,10},{10,1... | collective-permute-start | bytes 12296 | tf_op jit(solution)/shard_map/while/body/eval_jaxpr/ppermute | solution.py:48
  67.7 1.4 %collective-permute-start = (f32[2,1,512]{2,1,0:T(1,128)S(1)}, f32[2,1,512]{2,1,0:T(1,128)S(1)}, u32[]{:S(2)}, u32[]{:S(2)}) collective-permute-start(f32[2,1,512]{2,1,0:T(1,128)S(1)} %get-tuple-element.143), channel_id=1, source_target_pairs={{1,0},{2,1},{3,2},{4,3},{5,4},{6,5},{7,6},{0,7},{9,8},{10,9},{11,1... | collective-permute-start | bytes 12296 | tf_op jit(solution)/shard_map/while/body/eval_jaxpr/ppermute | solution.py:51
  67.7 4.0 %collective-permute-start.1 = (f32[2,1,512]{2,1,0:T(1,128)S(1)}, f32[2,1,512]{2,1,0:T(1,128)S(1)}, u32[]{:S(2)}, u32[]{:S(2)}) collective-permute-start(f32[2,1,512]{2,1,0:T(1,128)S(1)} %get-tuple-element.145), channel_id=1, source_target_pairs={{0,1},{1,2},{2,3},{3,4},{4,5},{5,6},{6,7},{7,0},{8,9},{9,10},{10,1... | collective-permute-start | bytes 12296 | tf_op jit(solution)/shard_map/while/body/eval_jaxpr/ppermute | solution.py:48
  71.9 1.4 %collective-permute-start = (f32[2,1,512]{2,1,0:T(1,128)S(1)}, f32[2,1,512]{2,1,0:T(1,128)S(1)}, u32[]{:S(2)}, u32[]{:S(2)}) collective-permute-start(f32[2,1,512]{2,1,0:T(1,128)S(1)} %get-tuple-element.143), channel_id=1, source_target_pairs={{1,0},{2,1},{3,2},{4,3},{5,4},{6,5},{7,6},{0,7},{9,8},{10,9},{11,1... | collective-permute-start | bytes 12296 | tf_op jit(solution)/shard_map/while/body/eval_jaxpr/ppermute | solution.py:51
  71.9 4.0 %collective-permute-start.1 = (f32[2,1,512]{2,1,0:T(1,128)S(1)}, f32[2,1,512]{2,1,0:T(1,128)S(1)}, u32[]{:S(2)}, u32[]{:S(2)}) collective-permute-start(f32[2,1,512]{2,1,0:T(1,128)S(1)} %get-tuple-element.145), channel_id=1, source_target_pairs={{0,1},{1,2},{2,3},{3,4},{4,5},{5,6},{6,7},{7,0},{8,9},{9,10},{10,1... | collective-permute-start | bytes 12296 | tf_op jit(solution)/shard_map/while/body/eval_jaxpr/ppermute | solution.py:48
